TPU v7x, 32 devices: a whole 2x2x4 slice. The times are simulated.
32 devices in a mesh: parts: 2 (over x), seq: 16 (over z, y, core).
Axes of the slice: x: 2, y: 2, z: 4, core: 2. Of those that a mesh axis runs over, the one named last changes fastest.
Arguments:
- x_state: bfloat16 [32, 64, 384], P(('parts', 'seq')), parts along dimension 0, may hold values from -6 to 6
- noise_field: bfloat16 [32, 64, 384], P(('parts', 'seq')), parts along dimension 0, may hold values from -6 to 6
- rotations: float32 [9, 32, 64], P(None, ('parts', 'seq')), parts along dimension 1, may hold values from -1 to 1, as said below
- translations: float32 [3, 32, 64], P(None, ('parts', 'seq')), parts along dimension 1, may hold values from -15 to 15
- residue_types: int32 [128], P('parts'), parts along dimension 0, may hold values from 0 to 20
- pocket_mask: int32 [128], P('parts'), parts along dimension 0, may hold values 0 or 1
- type_table: bfloat16 [21, 384], replicated, may hold values from -3 to 3
- null_embed: bfloat16 [384], replicated, may hold values from -3 to 3
- spatial_gain: float32 [384], replicated, may hold values from 0.25 to 1.75
- spatial_proj: bfloat16 [384, 1152], replicated, may hold values from -0.3125 to 0.3125
- spatial_points: bfloat16 [384, 288], replicated, may hold values from -0.3125 to 0.3125
- spatial_gamma: float32 [12], replicated, may hold values from 0.2 to 2
- spatial_out: bfloat16 [384, 384], replicated, may hold values from -0.3125 to 0.3125
- temporal_gain: float32 [384], replicated, may hold values from 0.25 to 1.75
- temporal_proj: bfloat16 [384, 1152], replicated, may hold values from -0.3125 to 0.3125
- temporal_out: bfloat16 [384, 384], replicated, may hold values from -0.3125 to 0.3125
- hidden_gain: float32 [384], replicated, may hold values from 0.25 to 1.75
- hidden_in: bfloat16 [384, 1536], replicated, may hold values from -0.3125 to 0.3125
- hidden_out: bfloat16 [1536, 384], replicated, may hold values from -0.15625 to 0.15625
- head_gain: float32 [384], replicated, may hold values from 0.25 to 1.75
- head_out: bfloat16 [384, 384], replicated, may hold values from -0.3125 to 0.3125
Outputs:
- x_next: bfloat16 [32, 64, 384], P(('parts', 'seq')), parts along dimension 0
- velocity: bfloat16 [32, 64, 384], P(('parts', 'seq')), parts along dimension 0
There are 2 independent parts, one for each index of `parts`. A program takes and returns all parts, laid end to end along the dimension named above; an argument that names none is the same for every part. Nothing has to cross between parts.
Inputs may be any that keep to these rules, and one draw needn't show every extreme that they name: `rotations`: each column over the first dimension is a proper rotation matrix, row-major.
All inputs are finite; a program needn't handle non-finite values.
Results may differ from a plain program's by a relative error of at most 0.015.
Values may be sent and summed in bfloat16 or wider, within the bound.
A program may use at most 64 MiB of HBM per device.

v0:
```python
import functools

import jax
import jax.numpy as jnp
from jax import lax
from jax.experimental import pallas as pl
from jax.experimental.pallas import tpu as pltpu
from jax.sharding import PartitionSpec as P

THEADS = 6
WEIGHT_LOGIT = 0.7071067811865476
WEIGHT_POINT = 0.23570226039551584
GUIDE = 2.0
STEP_SIZE = 0.25
NOISE_SCALE = 0.2
EPSILON = 1e-05
BLOCK = 16
INPUTS = 20
VMEM_BYTES = 66_300_000
FINISH_BYTES = 1 << 20
GELU_SCALE = 0.7978845608028654

F32 = jnp.float32
BF16 = jnp.bfloat16
MESH = pl.DeviceIdType.MESH


def layer_norm(values, gain):
    average = jnp.mean(values, axis=-1, keepdims=True)
    centered = values - average
    spread = jnp.mean(centered * centered, axis=-1, keepdims=True)
    return centered * lax.rsqrt(spread + EPSILON) * gain


def dot(a, b):
    return jnp.dot(a, b, preferred_element_type=F32)


def dot_nt(a, b):
    return lax.dot_general(a, b, (((1,), (1,)), ((), ())), preferred_element_type=F32)


def dot_tn(a, b):
    return lax.dot_general(a, b, (((0,), (0,)), ((), ())), preferred_element_type=F32)


def iota(shape, axis):
    return lax.broadcasted_iota(jnp.int32, shape, axis)


def softmax_down(logits):
    top = jnp.max(logits, axis=0, keepdims=True)
    powers = jnp.exp(logits - top)
    return (powers * (1.0 / jnp.sum(powers, axis=0, keepdims=True))).astype(BF16)


def split3(values):
    high = values.astype(BF16)
    rest = values - high.astype(F32)
    middle = rest.astype(BF16)
    low = (rest - middle.astype(F32)).astype(BF16)
    return high, middle, low


def kernel(n, *refs):
    sources, vel_ref, refs = refs[:INPUTS], refs[INPUTS], refs[INPUTS + 1 :]
    targets, refs = refs[:INPUTS], refs[INPUTS:]
    small, points, qfeat, kfeat, send1, recv1, send2, recv2, load_sem, s1, r1, s2, r2 = refs
    (x_ref, rot_ref, trans_ref, types_ref, mask_ref, table_ref, null_ref, sgain_ref, spts, sproj,
     gamma_ref, sout, tgain_ref, tproj, tout, hgain_ref, hin, hout, egain_ref, head) = targets
    me = lax.axis_index("seq")
    loads = [
        pltpu.make_async_copy(source, target, load_sem.at[index])
        for index, (source, target) in enumerate(zip(sources, targets))
    ]
    for load in loads:
        load.start()
    arrivals = iter(loads)

    def take(count):
        for _ in range(count):
            next(arrivals).wait()

    barrier = pltpu.get_barrier_semaphore()

    def greet(step, carry):
        pl.semaphore_signal(barrier, inc=1, device_id={"seq": lax.rem(me + step, n)}, device_id_type=MESH)
        return carry

    lax.fori_loop(1, n, greet, 0, unroll=True)

    _, residues, width = x_ref.shape
    share = residues // n
    group = 2 * share
    rows = 2 * residues
    shift_share = share.bit_length() - 1
    shift_group = group.bit_length() - 1
    sheads = gamma_ref.shape[0]
    head_dim = width // sheads
    npoints = spts.shape[0] // (6 * sheads)
    chunks = rows // points.shape[2]
    lanes = points.shape[2]

    def order(ids):
        return share * (ids >> shift_group) + (ids & (share - 1))

    take(8)
    trans = trans_ref[...].reshape(3, residues)
    small[...] = jnp.zeros_like(small)
    small[0:9, :] = rot_ref[...].reshape(9, residues)
    small[9:12, :] = trans - jnp.mean(trans, axis=1, keepdims=True)
    small[12:13, :] = mask_ref[...].astype(F32).reshape(1, residues)
    small[13:14, :] = types_ref[...].astype(F32).reshape(1, residues)
    spread = (iota((residues, rows), 0) == order(iota((residues, rows), 1))).astype(F32)
    table_rows = jnp.dot(small[...], spread, precision=lax.Precision.HIGHEST, preferred_element_type=F32)
    columns = jnp.concatenate([table_rows, jnp.zeros((128 - table_rows.shape[0], rows), F32)], axis=0).T

    gather = (iota((rows, residues), 1) == order(iota((rows, residues), 0))).astype(BF16)
    branch_col = (iota((rows, 1), 0) >> shift_share) & 1
    kinds = table_ref.shape[0]
    type_col = columns[:, 13:14].astype(jnp.int32)
    onehot = ((iota((rows, kinds), 1) == type_col) & (branch_col == 0)).astype(BF16)
    empty = jnp.where(branch_col == 1, null_ref[...].astype(F32).reshape(1, width), 0.0)
    initial = dot(gather, x_ref[0]) + (dot(onehot, table_ref[...]) + empty)
    normed = layer_norm(initial, sgain_ref[...].reshape(1, width)).astype(BF16)

    j_ids = iota((rows, rows), 0)
    i_ids = iota((rows, rows), 1)
    same_branch = ((j_ids >> shift_share) & 1) == ((i_ids >> shift_share) & 1)
    allowed = same_branch & ((columns[:, 12:13] == 1.0) | (j_ids == i_ids))
    bias = jnp.where(allowed, 0.0, -jnp.inf)

    take(1)
    pts = dot_nt(spts[...], normed)
    for c in range(chunks):
        points[c] = pts[:, c * lanes : (c + 1) * lanes]
    take(1)
    projected = dot(normed, sproj[...]).astype(BF16)
    turned = projected.T
    q_t = turned[:width] * BF16(WEIGHT_LOGIT / head_dim**0.5)
    k_t = turned[width : 2 * width]
    v_t = turned[2 * width :]

    take(1)
    eye = iota((sheads, sheads), 0) == iota((sheads, sheads), 1)
    gamma_col = jnp.sum(jnp.where(eye, gamma_ref[...].reshape(1, sheads), 0.0), axis=1, keepdims=True)
    weight_col = (WEIGHT_LOGIT * WEIGHT_POINT) * gamma_col
    ones = jnp.ones((sheads, lanes), F32)
    qfeat[...] = jnp.zeros_like(qfeat)
    kfeat[...] = jnp.zeros_like(kfeat)
    for c in range(chunks):
        frame = table_rows[:, c * lanes : (c + 1) * lanes]
        for side, feat in ((0, qfeat), (1, kfeat)):
            norm = jnp.zeros((sheads, lanes), F32)
            for p in range(npoints):
                local = [
                    points[c, pl.ds(side * sheads * npoints * 3 + p * 3 + e, sheads, stride=npoints * 3), :]
                    for e in range(3)
                ]
                for d in range(3):
                    placed = (
                        frame[3 * d : 3 * d + 1] * local[0]
                        + frame[3 * d + 1 : 3 * d + 2] * local[1]
                        + frame[3 * d + 2 : 3 * d + 3] * local[2]
                        + frame[9 + d : 10 + d]
                    )
                    norm = norm + placed * placed
                    feat[c, pl.ds(d * npoints + p, sheads, stride=BLOCK), :] = (
                        placed * weight_col if side == 0 else placed
                    )
            norm = norm * (-0.5 * weight_col)
            last = 3 * npoints
            feat[c, pl.ds(last, sheads, stride=BLOCK), :] = norm if side == 0 else ones
            feat[c, pl.ds(last + 1, sheads, stride=BLOCK), :] = ones if side == 0 else norm

    q_parts = split3(jnp.concatenate([qfeat[c] for c in range(chunks)], axis=1))
    k_parts = split3(jnp.concatenate([kfeat[c] for c in range(chunks)], axis=1))
    contexts = []
    for h in range(sheads):
        scalar = slice(h * head_dim, (h + 1) * head_dim)
        block = slice(h * BLOCK, (h + 1) * BLOCK)
        q_h = jnp.concatenate([q_t[scalar]] + [q_parts[t][block] for t in (0, 0, 1, 0, 2, 1)], axis=0)
        k_h = jnp.concatenate([k_t[scalar]] + [k_parts[t][block] for t in (0, 1, 0, 2, 0, 1)], axis=0)
        attend = softmax_down(dot_tn(k_h, q_h) + bias)
        contexts.append(dot(v_t[scalar], attend).astype(BF16))
    context = jnp.concatenate(contexts, axis=0).T
    take(1)
    state = initial + dot(context, sout[...])
    send1[...] = state.reshape(n, group, width).astype(BF16)

    pl.semaphore_wait(barrier, n - 1)

    bits = [lax.rem(me // 2**k, 2) for k in range((n - 1).bit_length())]

    def partner(step):
        return me + sum((1 - 2 * bit) * 2**k for k, bit in enumerate(bits) if (step >> k) & 1)

    def swap(source, target, send_sem, recv_sem):
        for step in range(n - 1, 0, -1):
            other = partner(step)
            pltpu.make_async_remote_copy(
                src_ref=source.at[other], dst_ref=target.at[me], send_sem=send_sem,
                recv_sem=recv_sem, device_id={"seq": other}, device_id_type=MESH,
            ).start()
        target[me] = source[me]
        pltpu.make_async_copy(target.at[pl.ds(0, n - 1)], target.at[pl.ds(0, n - 1)], recv_sem).wait()
        pltpu.make_async_copy(source.at[pl.ds(0, n - 1)], source.at[pl.ds(0, n - 1)], send_sem).wait()

    swap(send1, recv1, s1, r1)
    take(8)

    count = n * group
    state = recv1[...].astype(F32).reshape(count, width)
    normed = layer_norm(state, tgain_ref[...].reshape(1, width)).astype(BF16)
    projected = dot(normed, tproj[...]).astype(BF16)
    same = (iota((count, count), 0) & (group - 1)) == (iota((count, count), 1) & (group - 1))
    bias = jnp.where(same, 0.0, -jnp.inf)
    tdim = width // THEADS
    pair = 128 // tdim
    lane_head = iota((1, 128), 1) >> (tdim.bit_length() - 1)
    v_t = projected[:, 2 * width :].T
    logits = []
    for g in range(width // 128):
        q_g = projected[:, g * 128 : (g + 1) * 128] * BF16(tdim**-0.5)
        k_g = projected[:, width + g * 128 : width + (g + 1) * 128]
        q_g = jnp.concatenate([jnp.where(lane_head == part, q_g, BF16(0.0)) for part in range(pair)], axis=0)
        scores = dot_nt(k_g, q_g)
        logits += [scores[:, part * count : (part + 1) * count] + bias for part in range(pair)]
    tops = [jnp.max(part, axis=0, keepdims=True) for part in logits]
    powers = [jnp.exp(part - top) for part, top in zip(logits, tops)]
    totals = [jnp.sum(part, axis=0, keepdims=True) for part in powers]
    attends = [(part * (1.0 / total)).astype(BF16) for part, total in zip(powers, totals)]
    contexts = [
        dot(v_t[h * tdim : (h + 1) * tdim], attend).astype(BF16) for h, attend in enumerate(attends)
    ]
    context = jnp.concatenate(contexts, axis=0).T
    after = state + dot(context, tout[...])
    second = layer_norm(after, hgain_ref[...].reshape(1, width)).astype(BF16)
    hidden = dot(second, hin[...])
    hidden = 0.5 * hidden * (1.0 + jnp.tanh(GELU_SCALE * (hidden + 0.044715 * hidden * hidden * hidden)))
    mixed = (after + dot(hidden.astype(BF16), hout[...])).astype(BF16).astype(F32)
    normed = layer_norm(mixed, egain_ref[...].reshape(1, width)).astype(BF16)
    both = dot(normed, head[...]).reshape(n, group, width)
    guided = both[:, share:] + GUIDE * (both[:, :share] - both[:, share:])
    send2[...] = guided.astype(BF16)
    swap(send2, recv2, s2, r2)
    vel_ref[...] = recv2[...].astype(F32).reshape(residues, width).astype(BF16)


def finish_kernel(raw_ref, x_ref, noise_ref, next_ref, vel_ref):
    velocity = raw_ref[...]
    vel_ref[0] = velocity
    next_ref[0] = (
        x_ref[0].astype(F32) + STEP_SIZE * velocity.astype(F32) + NOISE_SCALE * noise_ref[0].astype(F32)
    ).astype(BF16)


def body(n, x_state, noise_field, rotations, translations, residue_types, pocket_mask, type_table,
         null_embed, spatial_gain, spatial_proj, spatial_points, spatial_gamma, spatial_out,
         temporal_gain, temporal_proj, temporal_out, hidden_gain, hidden_in, hidden_out,
         head_gain, head_out):
    _, residues, width = x_state.shape
    share = residues // n
    rows = 2 * residues
    sheads = spatial_gamma.shape[0]
    chunks = rows // 128
    inputs = [x_state, rotations, translations, residue_types, pocket_mask, type_table, null_embed,
              spatial_gain, spatial_points.T, spatial_proj, spatial_gamma, spatial_out,
              temporal_gain, temporal_proj, temporal_out, hidden_gain, hidden_in, hidden_out,
              head_gain, head_out]
    dma = pltpu.SemaphoreType.DMA
    velocity = pl.pallas_call(
        functools.partial(kernel, n),
        out_shape=pltpu.VMEM((residues, width), BF16),
        in_specs=[pl.BlockSpec(memory_space=pltpu.HBM)] * INPUTS,
        out_specs=pl.BlockSpec(memory_space=pltpu.VMEM),
        scratch_shapes=[pltpu.VMEM(w.shape, w.dtype) for w in inputs]
        + [
            pltpu.VMEM((16, residues), F32),
            pltpu.VMEM((chunks, spatial_points.shape[1], 128), F32),
            pltpu.VMEM((chunks, sheads * BLOCK, 128), F32),
            pltpu.VMEM((chunks, sheads * BLOCK, 128), F32),
            pltpu.VMEM((n, 2 * share, width), BF16),
            pltpu.VMEM((n, 2 * share, width), BF16),
            pltpu.VMEM((n, share, width), BF16),
            pltpu.VMEM((n, share, width), BF16),
            dma((INPUTS,)), dma, dma, dma, dma,
        ],
        compiler_params=pltpu.CompilerParams(
            collective_id=0, has_side_effects=True, vmem_limit_bytes=VMEM_BYTES
        ),
    )(*inputs)
    whole = pl.BlockSpec(memory_space=pltpu.VMEM)
    return pl.pallas_call(
        finish_kernel,
        out_shape=(jax.ShapeDtypeStruct(x_state.shape, BF16),) * 2,
        in_specs=[whole] * 3,
        out_specs=(whole, whole),
        compiler_params=pltpu.CompilerParams(vmem_limit_bytes=FINISH_BYTES),
    )(velocity, x_state, noise_field)


def solution(mesh):
    split = P(("parts", "seq"), None, None)
    frames = P(None, ("parts", "seq"), None)
    return jax.shard_map(
        functools.partial(body, mesh.shape["seq"]),
        mesh=mesh,
        in_specs=(split, split, frames, frames, P("parts"), P("parts")) + (P(),) * 15,
        out_specs=(split, split),
        check_vma=False,
    )
```

profile of v0, /device:TPU:0, one launch (start us, length us, event | category | flops | bytes accessed | tf_op | source)
XLA Modules:
  0.0 17.9 jit_solution(7737713219960548139)
XLA Ops:
  0.6 0.0 copy-start
  0.6 0.0 copy-start.1
  0.7 16.6 %shard_map.212.raw_ref = bf16[64,384]{1,0:T(8,128)(2,1)S(1)} custom-call(bf16[1,64,384]{2,1,0:T(8,128)(2,1)} %x_ref.1, f32[9,1,64]{2,1,0:T(1,128)} %refs_1_.1, f32[3,1,64]{2,1,0:T(1,128)} %refs_2_.1, s32[64]{0:T(128)} %refs_3_.1, s32[64]{0:T(128)} %refs_4_.1, bf16[21,384]{1,0:T(8,128)(2,1)} %refs_5_.1, bf16[384]{0:T(512)(128)(2,1)} %refs_6_.1, f32[384]{0:T(512)} %refs_7_.1, ...), custom_call_target="tpu_custom_call" | custom-call | tf_op jit(solution)/shard_map/pallas_call | solution.py:272
  17.3 0.0 copy-done
  17.3 0.0 copy-done.1
  17.3 0.7 %shard_map.213 = (bf16[1,64,384]{2,1,0:T(8,128)(2,1)}, bf16[1,64,384]{2,1,0:T(8,128)(2,1)}) custom-call(bf16[64,384]{1,0:T(8,128)(2,1)S(1)} %shard_map.212.raw_ref, bf16[1,64,384]{2,1,0:T(8,128)(2,1)S(1)} %copy-done, bf16[1,64,384]{2,1,0:T(8,128)(2,1)S(1)} %copy-done.1), custom_call_target="tpu_custom_call" | custom-call | tf_op jit(solution)/shard_map/pallas_call | solution.py:294
Async XLA Ops:
  0.6 16.6 %copy-start = (bf16[1,64,384]{2,1,0:T(8,128)(2,1)S(1)}, bf16[1,64,384]{2,1,0:T(8,128)(2,1)}, u32[]{:S(2)}) copy-start(bf16[1,64,384]{2,1,0:T(8,128)(2,1)} %x_ref.1) | copy-start | bytes 147460
  0.6 16.6 %copy-start.1 = (bf16[1,64,384]{2,1,0:T(8,128)(2,1)S(1)}, bf16[1,64,384]{2,1,0:T(8,128)(2,1)}, u32[]{:S(2)}) copy-start(bf16[1,64,384]{2,1,0:T(8,128)(2,1)} %noise_ref.1) | copy-start | bytes 147460
where the time goes:
time: 18.1 us; the launch traced here: 17.9 us
  Pallas kernels  17.3 us (96%)
  between operations  0.68 us (4%)
    pallas_call x1, Pallas kernels, body(): pl.pallas_call(functools.partial(kernel, n), out_shape=pltpu.VMEM((residu...  16.6 us
    pallas_call x1, Pallas kernels, body(): pl.pallas_call(finish_kernel, out_shape=(jax.ShapeDtypeStruct(x_state.sha...  0.65 us

commit v1 on v0

--- a/solution.py
+++ b/solution.py
@@ -48,10 +48,41 @@
     return lax.broadcasted_iota(jnp.int32, shape, axis)
 
 
+def fold(values, op):
+    rows = values.shape[0]
+    while rows > 8:
+        values = op(values[: rows // 2], values[rows // 2 :])
+        rows //= 2
+    return values
+
+
 def softmax_down(logits):
-    top = jnp.max(logits, axis=0, keepdims=True)
-    powers = jnp.exp(logits - top)
-    return (powers * (1.0 / jnp.sum(powers, axis=0, keepdims=True))).astype(BF16)
+    powers = jnp.exp(logits - jnp.max(fold(logits, jnp.maximum), axis=0, keepdims=True))
+    return powers.astype(BF16), 1.0 / jnp.sum(fold(powers, jnp.add), axis=0, keepdims=True)
+
+
+def interleave(first, second, share):
+    rows, width = first.shape
+    if 2 * share != 8:
+        parts = [part.reshape(rows // share, share, width) for part in (first, second)]
+        return jnp.concatenate(parts, axis=1)
+    first, second = first.reshape(rows // 8, 8, width), second.reshape(rows // 8, 8, width)
+    low = iota(first.shape, 1) < share
+    even = jnp.where(low, first, pltpu.roll(second, share, 1))
+    odd = jnp.where(low, pltpu.roll(first, share, 1), second)
+    return jnp.stack([even, odd], axis=1).reshape(rows // share, 8, width)
+
+
+def guide(both, share):
+    n, group, width = both.shape
+    if group != 8:
+        return both[:, share:] + GUIDE * (both[:, :share] - both[:, share:])
+    both = both.reshape(n // 2, 2, 8, width)
+    even, odd = both[:, 0], both[:, 1]
+    low = iota(even.shape, 1) < share
+    first = jnp.where(low, even, pltpu.roll(odd, share, 1))
+    second = jnp.where(low, pltpu.roll(even, share, 1), odd)
+    return (second + GUIDE * (first - second)).reshape(n, share, width)
 
 
 def split3(values):
@@ -65,7 +96,7 @@
 def kernel(n, *refs):
     sources, vel_ref, refs = refs[:INPUTS], refs[INPUTS], refs[INPUTS + 1 :]
     targets, refs = refs[:INPUTS], refs[INPUTS:]
-    small, points, qfeat, kfeat, send1, recv1, send2, recv2, load_sem, s1, r1, s2, r2 = refs
+    points, qfeat, kfeat, send1, recv1, send2, recv2, load_sem, s1, r1, s2, r2 = refs
     (x_ref, rot_ref, trans_ref, types_ref, mask_ref, table_ref, null_ref, sgain_ref, spts, sproj,
      gamma_ref, sout, tgain_ref, tproj, tout, hgain_ref, hin, hout, egain_ref, head) = targets
     me = lax.axis_index("seq")
@@ -93,42 +124,34 @@
     share = residues // n
     group = 2 * share
     rows = 2 * residues
-    shift_share = share.bit_length() - 1
-    shift_group = group.bit_length() - 1
     sheads = gamma_ref.shape[0]
     head_dim = width // sheads
     npoints = spts.shape[0] // (6 * sheads)
     chunks = rows // points.shape[2]
     lanes = points.shape[2]
 
-    def order(ids):
-        return share * (ids >> shift_group) + (ids & (share - 1))
-
     take(8)
     trans = trans_ref[...].reshape(3, residues)
-    small[...] = jnp.zeros_like(small)
-    small[0:9, :] = rot_ref[...].reshape(9, residues)
-    small[9:12, :] = trans - jnp.mean(trans, axis=1, keepdims=True)
-    small[12:13, :] = mask_ref[...].astype(F32).reshape(1, residues)
-    small[13:14, :] = types_ref[...].astype(F32).reshape(1, residues)
-    spread = (iota((residues, rows), 0) == order(iota((residues, rows), 1))).astype(F32)
-    table_rows = jnp.dot(small[...], spread, precision=lax.Precision.HIGHEST, preferred_element_type=F32)
-    columns = jnp.concatenate([table_rows, jnp.zeros((128 - table_rows.shape[0], rows), F32)], axis=0).T
-
-    gather = (iota((rows, residues), 1) == order(iota((rows, residues), 0))).astype(BF16)
-    branch_col = (iota((rows, 1), 0) >> shift_share) & 1
+    trans = trans - jnp.mean(trans, axis=1, keepdims=True)
+    frames = jnp.concatenate([rot_ref[...].reshape(9, residues), trans], axis=0)
+    frames = jnp.concatenate([frames, frames], axis=1)
+
     kinds = table_ref.shape[0]
-    type_col = columns[:, 13:14].astype(jnp.int32)
-    onehot = ((iota((rows, kinds), 1) == type_col) & (branch_col == 0)).astype(BF16)
-    empty = jnp.where(branch_col == 1, null_ref[...].astype(F32).reshape(1, width), 0.0)
-    initial = dot(gather, x_ref[0]) + (dot(onehot, table_ref[...]) + empty)
+    types_row = types_ref[...].astype(F32).reshape(1, residues)
+    onehot = (iota((kinds, residues), 0).astype(F32) == types_row).astype(BF16)
+    x_rows = x_ref[0].astype(F32)
+    initial = jnp.concatenate(
+        [x_rows + dot_tn(onehot, table_ref[...]), x_rows + null_ref[...].astype(F32).reshape(1, width)], axis=0
+    )
     normed = layer_norm(initial, sgain_ref[...].reshape(1, width)).astype(BF16)
 
-    j_ids = iota((rows, rows), 0)
-    i_ids = iota((rows, rows), 1)
-    same_branch = ((j_ids >> shift_share) & 1) == ((i_ids >> shift_share) & 1)
-    allowed = same_branch & ((columns[:, 12:13] == 1.0) | (j_ids == i_ids))
-    bias = jnp.where(allowed, 0.0, -jnp.inf)
+    j_ids = iota((residues, residues), 0)
+    i_ids = iota((residues, residues), 1)
+    mask_row = mask_ref[...].astype(F32).reshape(1, residues)
+    mask_col = jnp.sum(jnp.where(j_ids == i_ids, mask_row, 0.0), axis=1, keepdims=True)
+    bias = jnp.where((mask_col == 1.0) | (j_ids == i_ids), 0.0, -jnp.inf)
+    bias = jnp.concatenate([bias, bias], axis=1)
+    left = iota((residues, rows), 1) < residues
 
     take(1)
     pts = dot_nt(spts[...], normed)
@@ -149,7 +172,7 @@
     qfeat[...] = jnp.zeros_like(qfeat)
     kfeat[...] = jnp.zeros_like(kfeat)
     for c in range(chunks):
-        frame = table_rows[:, c * lanes : (c + 1) * lanes]
+        frame = frames[:, c * lanes : (c + 1) * lanes]
         for side, feat in ((0, qfeat), (1, kfeat)):
             norm = jnp.zeros((sheads, lanes), F32)
             for p in range(npoints):
@@ -181,12 +204,23 @@
         block = slice(h * BLOCK, (h + 1) * BLOCK)
         q_h = jnp.concatenate([q_t[scalar]] + [q_parts[t][block] for t in (0, 0, 1, 0, 2, 1)], axis=0)
         k_h = jnp.concatenate([k_t[scalar]] + [k_parts[t][block] for t in (0, 1, 0, 2, 0, 1)], axis=0)
-        attend = softmax_down(dot_tn(k_h, q_h) + bias)
-        contexts.append(dot(v_t[scalar], attend).astype(BF16))
+        v_h = v_t[scalar]
+        if residues % 128:
+            scores = dot_tn(k_h, q_h)
+            attend, inverse = softmax_down(jnp.where(left, scores[:residues], scores[residues:]) + bias)
+            blank = jnp.zeros_like(attend)
+            attend = jnp.concatenate([jnp.where(left, attend, blank), jnp.where(left, blank, attend)], axis=0)
+            contexts.append((dot(v_h, attend) * inverse).astype(BF16))
+        else:
+            halves = [slice(b * residues, (b + 1) * residues) for b in range(2)]
+            scores = jnp.concatenate([dot_tn(k_h[:, half], q_h[:, half]) for half in halves], axis=1)
+            attend, inverse = softmax_down(scores + bias)
+            mixed = jnp.concatenate([dot(v_h[:, half], attend[:, half]) for half in halves], axis=1)
+            contexts.append((mixed * inverse).astype(BF16))
     context = jnp.concatenate(contexts, axis=0).T
     take(1)
     state = initial + dot(context, sout[...])
-    send1[...] = state.reshape(n, group, width).astype(BF16)
+    send1[...] = interleave(state[:residues], state[residues:], share).astype(BF16)
 
     pl.semaphore_wait(barrier, n - 1)
 
@@ -204,7 +238,6 @@
             ).start()
         target[me] = source[me]
         pltpu.make_async_copy(target.at[pl.ds(0, n - 1)], target.at[pl.ds(0, n - 1)], recv_sem).wait()
-        pltpu.make_async_copy(source.at[pl.ds(0, n - 1)], source.at[pl.ds(0, n - 1)], send_sem).wait()
 
     swap(send1, recv1, s1, r1)
     take(8)
@@ -226,25 +259,25 @@
         q_g = jnp.concatenate([jnp.where(lane_head == part, q_g, BF16(0.0)) for part in range(pair)], axis=0)
         scores = dot_nt(k_g, q_g)
         logits += [scores[:, part * count : (part + 1) * count] + bias for part in range(pair)]
-    tops = [jnp.max(part, axis=0, keepdims=True) for part in logits]
-    powers = [jnp.exp(part - top) for part, top in zip(logits, tops)]
-    totals = [jnp.sum(part, axis=0, keepdims=True) for part in powers]
-    attends = [(part * (1.0 / total)).astype(BF16) for part, total in zip(powers, totals)]
+    attends = [softmax_down(part) for part in logits]
     contexts = [
-        dot(v_t[h * tdim : (h + 1) * tdim], attend).astype(BF16) for h, attend in enumerate(attends)
+        (dot(v_t[h * tdim : (h + 1) * tdim], attend) * inverse).astype(BF16)
+        for h, (attend, inverse) in enumerate(attends)
     ]
     context = jnp.concatenate(contexts, axis=0).T
     after = state + dot(context, tout[...])
     second = layer_norm(after, hgain_ref[...].reshape(1, width)).astype(BF16)
     hidden = dot(second, hin[...])
-    hidden = 0.5 * hidden * (1.0 + jnp.tanh(GELU_SCALE * (hidden + 0.044715 * hidden * hidden * hidden)))
-    mixed = (after + dot(hidden.astype(BF16), hout[...])).astype(BF16).astype(F32)
+    inner = hidden * (GELU_SCALE + (GELU_SCALE * 0.044715) * (hidden * hidden))
+    doubled = (hidden + hidden * jnp.tanh(inner)).astype(BF16)
+    mixed = (after + 0.5 * dot(doubled, hout[...])).astype(BF16).astype(F32)
     normed = layer_norm(mixed, egain_ref[...].reshape(1, width)).astype(BF16)
     both = dot(normed, head[...]).reshape(n, group, width)
-    guided = both[:, share:] + GUIDE * (both[:, :share] - both[:, share:])
-    send2[...] = guided.astype(BF16)
+    send2[...] = guide(both, share).astype(BF16)
     swap(send2, recv2, s2, r2)
     vel_ref[...] = recv2[...].astype(F32).reshape(residues, width).astype(BF16)
+    for source, sem in ((send1, s1), (send2, s2)):
+        pltpu.make_async_copy(source.at[pl.ds(0, n - 1)], source.at[pl.ds(0, n - 1)], sem).wait()
 
 
 def finish_kernel(raw_ref, x_ref, noise_ref, next_ref, vel_ref):
@@ -276,7 +309,6 @@
         out_specs=pl.BlockSpec(memory_space=pltpu.VMEM),
         scratch_shapes=[pltpu.VMEM(w.shape, w.dtype) for w in inputs]
         + [
-            pltpu.VMEM((16, residues), F32),
             pltpu.VMEM((chunks, spatial_points.shape[1], 128), F32),
             pltpu.VMEM((chunks, sheads * BLOCK, 128), F32),
             pltpu.VMEM((chunks, sheads * BLOCK, 128), F32),

time: 18.1 us -> 18 us (level)
  Pallas kernels: 17.3 us -> 17.1 us
where the time goes in v1:
time: 18 us; the launch traced here: 17.8 us
  Pallas kernels  17.1 us (95%)
  between operations  0.68 us (4%)
    pallas_call x1, Pallas kernels, body(): pl.pallas_call(functools.partial(kernel, n), out_shape=pltpu.VMEM((residu...  16.5 us
    pallas_call x1, Pallas kernels, body(): pl.pallas_call(finish_kernel, out_shape=(jax.ShapeDtypeStruct(x_state.sha...  0.65 us

profile of v1, /device:TPU:0, one launch (start us, length us, event | category | flops | bytes accessed | tf_op | source)
XLA Modules:
  0.0 17.8 jit_solution(566949905198321910)
XLA Ops:
  0.6 0.0 copy-start
  0.6 0.0 copy-start.1
  0.7 16.5 %shard_map.212.raw_ref = bf16[64,384]{1,0:T(8,128)(2,1)S(1)} custom-call(bf16[1,64,384]{2,1,0:T(8,128)(2,1)} %x_ref.1, f32[9,1,64]{2,1,0:T(1,128)} %refs_1_.1, f32[3,1,64]{2,1,0:T(1,128)} %refs_2_.1, s32[64]{0:T(128)} %refs_3_.1, s32[64]{0:T(128)} %refs_4_.1, bf16[21,384]{1,0:T(8,128)(2,1)} %refs_5_.1, bf16[384]{0:T(512)(128)(2,1)} %refs_6_.1, f32[384]{0:T(512)} %refs_7_.1, ...), custom_call_target="tpu_custom_call" | custom-call | tf_op jit(solution)/shard_map/pallas_call | solution.py:305
  17.2 0.0 copy-done
  17.2 0.0 copy-done.1
  17.2 0.7 %shard_map.213 = (bf16[1,64,384]{2,1,0:T(8,128)(2,1)}, bf16[1,64,384]{2,1,0:T(8,128)(2,1)}) custom-call(bf16[64,384]{1,0:T(8,128)(2,1)S(1)} %shard_map.212.raw_ref, bf16[1,64,384]{2,1,0:T(8,128)(2,1)S(1)} %copy-done, bf16[1,64,384]{2,1,0:T(8,128)(2,1)S(1)} %copy-done.1), custom_call_target="tpu_custom_call" | custom-call | tf_op jit(solution)/shard_map/pallas_call | solution.py:326
Async XLA Ops:
  0.6 16.5 %copy-start = (bf16[1,64,384]{2,1,0:T(8,128)(2,1)S(1)}, bf16[1,64,384]{2,1,0:T(8,128)(2,1)}, u32[]{:S(2)}) copy-start(bf16[1,64,384]{2,1,0:T(8,128)(2,1)} %x_ref.1) | copy-start | bytes 147460
  0.6 16.5 %copy-start.1 = (bf16[1,64,384]{2,1,0:T(8,128)(2,1)S(1)}, bf16[1,64,384]{2,1,0:T(8,128)(2,1)}, u32[]{:S(2)}) copy-start(bf16[1,64,384]{2,1,0:T(8,128)(2,1)} %noise_ref.1) | copy-start | bytes 147460

commit v2 on v1

--- a/solution.py
+++ b/solution.py
@@ -96,7 +96,7 @@
 def kernel(n, *refs):
     sources, vel_ref, refs = refs[:INPUTS], refs[INPUTS], refs[INPUTS + 1 :]
     targets, refs = refs[:INPUTS], refs[INPUTS:]
-    points, qfeat, kfeat, send1, recv1, send2, recv2, load_sem, s1, r1, s2, r2 = refs
+    points, qfeat, kfeat, send1, recv1, send2, recv2, saved, load_sem, s1, r1, s2, r2 = refs
     (x_ref, rot_ref, trans_ref, types_ref, mask_ref, table_ref, null_ref, sgain_ref, spts, sproj,
      gamma_ref, sout, tgain_ref, tproj, tout, hgain_ref, hin, hout, egain_ref, head) = targets
     me = lax.axis_index("seq")
@@ -265,16 +265,40 @@
         for h, (attend, inverse) in enumerate(attends)
     ]
     context = jnp.concatenate(contexts, axis=0).T
-    after = state + dot(context, tout[...])
-    second = layer_norm(after, hgain_ref[...].reshape(1, width)).astype(BF16)
-    hidden = dot(second, hin[...])
-    inner = hidden * (GELU_SCALE + (GELU_SCALE * 0.044715) * (hidden * hidden))
-    doubled = (hidden + hidden * jnp.tanh(inner)).astype(BF16)
-    mixed = (after + 0.5 * dot(doubled, hout[...])).astype(BF16).astype(F32)
-    normed = layer_norm(mixed, egain_ref[...].reshape(1, width)).astype(BF16)
-    both = dot(normed, head[...]).reshape(n, group, width)
-    send2[...] = guide(both, share).astype(BF16)
-    swap(send2, recv2, s2, r2)
+    saved[...] = context
+
+    def finish_rows(first, last):
+        frames_in = slice(first // group, last // group)
+        state = recv1[frames_in].astype(F32).reshape(last - first, width)
+        after = state + dot(saved[first:last], tout[...])
+        second = layer_norm(after, hgain_ref[...].reshape(1, width)).astype(BF16)
+        hidden = dot(second, hin[...])
+        inner = hidden * (GELU_SCALE + (GELU_SCALE * 0.044715) * (hidden * hidden))
+        doubled = (hidden + hidden * jnp.tanh(inner)).astype(BF16)
+        mixed = (after + 0.5 * dot(doubled, hout[...])).astype(BF16).astype(F32)
+        normed = layer_norm(mixed, egain_ref[...].reshape(1, width)).astype(BF16)
+        both = dot(normed, head[...]).reshape((last - first) // group, group, width)
+        send2[frames_in] = guide(both, share).astype(BF16)
+
+    def reply(device):
+        pltpu.make_async_remote_copy(
+            src_ref=send2.at[device], dst_ref=recv2.at[me], send_sem=s2,
+            recv_sem=r2, device_id={"seq": device}, device_id_type=MESH,
+        ).start()
+
+    finish_rows(0, 2 * group)
+    for device in range(2):
+        pl.when(me != device)(functools.partial(reply, device))
+
+    @pl.when(me < n)
+    def _():
+        finish_rows(2 * group, count)
+
+    for step in range(2, n - 1):
+        reply(step + ((me >= 2) & (step >= me)).astype(jnp.int32))
+    pl.when(me < 2)(functools.partial(reply, n - 1))
+    recv2[me] = send2[me]
+    pltpu.make_async_copy(recv2.at[pl.ds(0, n - 1)], recv2.at[pl.ds(0, n - 1)], r2).wait()
     vel_ref[...] = recv2[...].astype(F32).reshape(residues, width).astype(BF16)
     for source, sem in ((send1, s1), (send2, s2)):
         pltpu.make_async_copy(source.at[pl.ds(0, n - 1)], source.at[pl.ds(0, n - 1)], sem).wait()
@@ -316,6 +340,7 @@
             pltpu.VMEM((n, 2 * share, width), BF16),
             pltpu.VMEM((n, share, width), BF16),
             pltpu.VMEM((n, share, width), BF16),
+            pltpu.VMEM((2 * residues, width), BF16),
             dma((INPUTS,)), dma, dma, dma, dma,
         ],
         compiler_params=pltpu.CompilerParams(

time: 18 us -> 17.8 us (0.989)
    pallas_call x1, Pallas kernels: 16.5 us -> 16.3 us  [body(): pl.pallas_call(functools.partial(kernel, n), out_shape=pltpu.VMEM((residu...]
where the time goes in v2:
time: 17.8 us; the launch traced here: 17.6 us
  Pallas kernels  17 us (96%)
  between operations  0.68 us (4%)
    pallas_call x1, Pallas kernels, body(): pl.pallas_call(functools.partial(kernel, n), out_shape=pltpu.VMEM((residu...  16.3 us
    pallas_call x1, Pallas kernels, body(): pl.pallas_call(finish_kernel, out_shape=(jax.ShapeDtypeStruct(x_state.sha...  0.65 us

profile of v2, /device:TPU:0, one launch (start us, length us, event | category | flops | bytes accessed | tf_op | source)
XLA Modules:
  0.0 17.6 jit_solution(15926524807776482150)
XLA Ops:
  0.6 0.0 copy-start
  0.6 0.0 copy-start.1
  0.7 16.3 %shard_map.212.raw_ref = bf16[64,384]{1,0:T(8,128)(2,1)S(1)} custom-call(bf16[1,64,384]{2,1,0:T(8,128)(2,1)} %x_ref.1, f32[9,1,64]{2,1,0:T(1,128)} %refs_1_.1, f32[3,1,64]{2,1,0:T(1,128)} %refs_2_.1, s32[64]{0:T(128)} %refs_3_.1, s32[64]{0:T(128)} %refs_4_.1, bf16[21,384]{1,0:T(8,128)(2,1)} %refs_5_.1, bf16[384]{0:T(512)(128)(2,1)} %refs_6_.1, f32[384]{0:T(512)} %refs_7_.1, ...), custom_call_target="tpu_custom_call" | custom-call | tf_op jit(solution)/shard_map/pallas_call | solution.py:329
  17.0 0.0 copy-done
  17.0 0.0 copy-done.1
  17.0 0.7 %shard_map.213 = (bf16[1,64,384]{2,1,0:T(8,128)(2,1)}, bf16[1,64,384]{2,1,0:T(8,128)(2,1)}) custom-call(bf16[64,384]{1,0:T(8,128)(2,1)S(1)} %shard_map.212.raw_ref, bf16[1,64,384]{2,1,0:T(8,128)(2,1)S(1)} %copy-done, bf16[1,64,384]{2,1,0:T(8,128)(2,1)S(1)} %copy-done.1), custom_call_target="tpu_custom_call" | custom-call | tf_op jit(solution)/shard_map/pallas_call | solution.py:351
Async XLA Ops:
  0.6 16.3 %copy-start = (bf16[1,64,384]{2,1,0:T(8,128)(2,1)S(1)}, bf16[1,64,384]{2,1,0:T(8,128)(2,1)}, u32[]{:S(2)}) copy-start(bf16[1,64,384]{2,1,0:T(8,128)(2,1)} %x_ref.1) | copy-start | bytes 147460
  0.6 16.3 %copy-start.1 = (bf16[1,64,384]{2,1,0:T(8,128)(2,1)S(1)}, bf16[1,64,384]{2,1,0:T(8,128)(2,1)}, u32[]{:S(2)}) copy-start(bf16[1,64,384]{2,1,0:T(8,128)(2,1)} %noise_ref.1) | copy-start | bytes 147460
